TPU v7x, 32 devices: a whole 2x2x4 slice. The times are simulated.
32 devices in a mesh: req: 8 (over z, x), head: 4 (over y, core).
Axes of the slice: x: 2, y: 2, z: 4, core: 2. Of those that a mesh axis runs over, the one named last changes fastest.
Arguments:
- hidden_state: bfloat16 [64, 2048], P('req'), may hold values from -6 to 6
- attend_gain: float32 [2048], replicated, may hold values from 0.1 to 1.9
- input_weight: bfloat16 [2048, 3, 2048], P(None, None, 'head'), may hold values from -0.125 to 0.125
- input_bias: float32 [3, 2048], P(None, 'head'), may hold values from -3 to 3
- output_weight: bfloat16 [2048, 2048], P('head'), may hold values from -0.125 to 0.125
- window_cache: bfloat16 [64, 2, 2048, 2048], P('req', None, None, 'head'), may hold values from -9 to 9
- sink_cache: bfloat16 [64, 2, 4, 2048], P('req', None, None, 'head'), may hold values from -3000 to 3000
- lengths: int32 [64], P('req'), may hold values from 16 to 32768, as said below
- expert_index: int32 [64, 4], P('req'), may hold values from 0 to 31, all different within a row; in each aligned block of 8 rows (0 to 7, 8 to 15, ...) at most 2 rows name the same one
- router_weight: float32 [64, 4], P('req'), may hold values from 0.05 to 0.5
- mixture_gain: float32 [2048], replicated, may hold values from 0.1 to 1.9
- expert_gate_up: bfloat16 [2, 45056, 2048], P(None, ('req', 'head')), may hold values from -0.125 to 0.125
- expert_down: bfloat16 [45056, 2048], P(('req', 'head')), may hold values from -0.3125 to 0.3125
- shared_gate_up: bfloat16 [2, 2048, 5632], P(None, 'req', 'head'), may hold values from -0.125 to 0.125
- shared_down: bfloat16 [5632, 2048], P('head', 'req'), may hold values from -0.078125 to 0.078125
- shared_gate: float32 [2048], replicated, may hold values from -0.125 to 0.125
Outputs:
- layer_out: bfloat16 [64, 2048], P('req', 'head')
- new_kv: bfloat16 [64, 2, 2048], P('req', None, 'head')
Inputs may be any that keep to these rules, and one draw needn't show every extreme that they name: Request r has lengths[r] cached tokens and its new token takes position lengths[r]; some request has exactly 32768 cached tokens and some has 16. `expert_index`: each row names 4 different experts; within the rows of one index of req (aligned blocks of 8 rows) no expert is named more than 2 times, a bound that some block reaches.
All inputs are finite; a program needn't handle non-finite values.
Results may differ from a plain program's by a relative error of at most 0.014.
The roundings to bfloat16 on the way count: a program that leaves them out, or rounds other values in their place, can miss the bound.
Values may be sent and summed in bfloat16 or wider, within the bound.
No kernel may reach another device: no remote copies, remote signals or barrier semaphores. Data moves between devices by JAX's collectives and lax.ppermute only.
A program may use at most 256 MiB of HBM per device.

v0:
```python
import math
import jax
import jax.numpy as jnp
from jax import lax
from jax.sharding import PartitionSpec as P

HD = 128
EXPERTS = 32
FE = 1408
SINKS = 4
CAP = 2
EPSILON = 1e-06
ROPE_BASE = 1000000.0


def rms_scale(values, gains):
    mean_square = jnp.mean(values * values, axis=-1, keepdims=True)
    return values * lax.rsqrt(mean_square + EPSILON) * gains


def rotate(vectors, positions):
    half_depth = vectors.shape[-1] // 2
    steps_half = jnp.arange(half_depth).astype(jnp.float32)
    frequencies = jnp.float32(ROPE_BASE) ** (-(2.0 / vectors.shape[-1]) * steps_half)
    angles = positions.astype(jnp.float32)[:, None] * frequencies[None, :]
    cosine = jnp.cos(angles)[:, None, :]
    sine_terms = jnp.sin(angles)[:, None, :]
    lower_half = vectors[..., :half_depth]
    upper_half = vectors[..., half_depth:]
    return jnp.concatenate(
        [
            lower_half * cosine - upper_half * sine_terms,
            upper_half * cosine + lower_half * sine_terms,
        ],
        axis=-1,
    )


def block_scores(queries, fresh_key, window_cache, fresh_slot, live_count, block_size):
    row_count, head_count, head_depth = queries.shape
    key_rows = window_cache[:, 0].reshape(row_count, block_size, head_count, head_depth)
    scores = jnp.einsum("rhd,rshd->rhs", queries, key_rows, preferred_element_type=jnp.float32)
    fresh_scores = jnp.einsum("rhd,rhd->rh", queries, fresh_key, preferred_element_type=jnp.float32)
    positions = jnp.arange(block_size)
    is_fresh = positions[None, :] == fresh_slot[:, None]
    scores = jnp.where(is_fresh[:, None, :], fresh_scores[:, :, None], scores) / math.sqrt(
        head_depth
    )
    keeping = positions[None, :] < live_count[:, None]
    return jnp.where(keeping[:, None, :], scores, -jnp.inf)


def block_values(window_cache, block_size, head_count, head_depth):
    row_count = window_cache.shape[0]
    return window_cache[:, 1].reshape(row_count, block_size, head_count, head_depth)


def window_values(weights, is_fresh, value_rows, fresh_value):
    kept_weights = jnp.where(is_fresh[:, None, :], jnp.zeros_like(weights), weights)
    fresh_weight = jnp.sum(
        jnp.where(is_fresh[:, None, :], weights, jnp.zeros_like(weights)), axis=-1
    )
    window_part = jnp.einsum(
        "rhs,rshd->rhd", kept_weights, value_rows, preferred_element_type=jnp.float32
    )
    return window_part + fresh_weight.astype(jnp.float32)[..., None] * fresh_value.astype(
        jnp.float32
    )


def expert_slice(arrived, expert_gate_up, expert_down):
    gate_terms = jnp.einsum(
        "nkd,fd->nkf", arrived, expert_gate_up[0], preferred_element_type=jnp.float32
    )
    up_terms = jnp.einsum(
        "nkd,fd->nkf", arrived, expert_gate_up[1], preferred_element_type=jnp.float32
    )
    hidden_units = (jax.nn.silu(gate_terms) * up_terms).astype(jnp.bfloat16)
    return jnp.einsum("nkf,fd->nkd", hidden_units, expert_down, preferred_element_type=jnp.float32)


def local(
    hidden_state,
    attend_gain,
    input_weight,
    input_bias,
    output_weight,
    window_cache,
    sink_cache,
    lengths,
    expert_index,
    router_weight,
    mixture_gain,
    expert_gate_up,
    expert_down,
    shared_gate_up,
    shared_down,
    shared_gate,
):
    row_count, model_width = hidden_state.shape
    local_width = input_weight.shape[2]
    head_depth = HD
    head_count = local_width // head_depth
    window_length = window_cache.shape[2]
    normed = rms_scale(hidden_state.astype(jnp.float32), attend_gain).astype(jnp.bfloat16)
    projected = jnp.dot(
        normed,
        input_weight.reshape(model_width, 3 * local_width),
        preferred_element_type=jnp.float32,
    ) + input_bias.reshape(3 * local_width)
    projected = projected.reshape(row_count, 3, head_count, head_depth)
    queries = rotate(projected[:, 0], lengths).astype(jnp.bfloat16)
    fresh_key = rotate(projected[:, 1], lengths).astype(jnp.bfloat16)
    fresh_value = projected[:, 2].astype(jnp.bfloat16)
    new_kv = jnp.stack(
        [fresh_key.reshape(row_count, local_width), fresh_value.reshape(row_count, local_width)],
        axis=1,
    )
    fresh_slot = (lengths - SINKS) % window_length
    live_count = jnp.minimum(lengths - SINKS + 1, window_length)
    sink_keys = sink_cache[:, 0].reshape(row_count, SINKS, head_count, head_depth)
    sink_values = sink_cache[:, 1].reshape(row_count, SINKS, head_count, head_depth)
    sink_scores = jnp.einsum(
        "rhd,rshd->rhs", queries, sink_keys, preferred_element_type=jnp.float32
    ) / math.sqrt(head_depth)
    scores = block_scores(queries, fresh_key, window_cache, fresh_slot, live_count, window_length)
    is_fresh = jnp.arange(window_length)[None, :] == fresh_slot[:, None]
    value_rows = block_values(window_cache, window_length, head_count, head_depth)
    score_peak = jnp.maximum(jnp.max(sink_scores, axis=-1), jnp.max(scores, axis=-1))
    window_exp = jnp.exp(scores - score_peak[..., None])
    score_total = jnp.sum(jnp.exp(sink_scores - score_peak[..., None]), axis=-1) + jnp.sum(
        window_exp, axis=-1
    )
    weights = (window_exp / score_total[..., None]).astype(jnp.bfloat16)
    accum = window_values(weights, is_fresh, value_rows, fresh_value)
    sink_weights = (jnp.exp(sink_scores - score_peak[..., None]) / score_total[..., None]).astype(
        jnp.bfloat16
    )
    accum = accum + jnp.einsum(
        "rhs,rshd->rhd", sink_weights, sink_values, preferred_element_type=jnp.float32
    )
    attended = accum.astype(jnp.bfloat16).reshape(row_count, local_width)
    attend_part = jnp.dot(attended, output_weight, preferred_element_type=jnp.float32)
    resid = hidden_state.astype(jnp.float32) + lax.psum(attend_part, "head")
    tokens = rms_scale(resid, mixture_gain).astype(jnp.bfloat16)
    all_tokens = lax.all_gather(tokens, "req", axis=0, tiled=True)
    group_index = lax.axis_index("req")
    group_count = lax.axis_size("req")
    row_width = shared_gate_up.shape[1]
    my_columns = lax.dynamic_slice_in_dim(all_tokens, group_index * row_width, row_width, 1)
    shared_terms = jnp.einsum(
        "td,cdf->ctf", my_columns, shared_gate_up, preferred_element_type=jnp.float32
    )
    shared_terms = lax.psum(shared_terms, "req")
    shared_hidden = (jax.nn.silu(shared_terms[0]) * shared_terms[1]).astype(jnp.bfloat16)
    gate_value = jax.nn.sigmoid(
        jnp.dot(all_tokens.astype(jnp.float32), shared_gate, precision=lax.Precision.HIGHEST)
    )
    shared_out = gate_value[:, None] * jnp.dot(
        shared_hidden, shared_down, preferred_element_type=jnp.float32
    )
    expert_hot = (expert_index[:, :, None] == jnp.arange(EXPERTS)[None, None, :]).astype(
        jnp.float32
    )
    combine = jnp.sum(expert_hot * router_weight[:, :, None], axis=1)
    local_experts = EXPERTS // group_count
    quarters = FE // expert_down.shape[0]
    local_pick = lax.axis_index("head") // quarters
    expert_hit = jnp.sum(expert_hot, axis=1)
    slot_rank = jnp.cumsum(expert_hit, axis=0) - expert_hit
    chosen = expert_hit[:, :, None] * (
        slot_rank[:, :, None] == jnp.arange(CAP)[None, None, :]
    ).astype(jnp.float32)
    mine_hot = (jnp.arange(local_experts) == local_pick).astype(jnp.float32)
    chosen_mine = jnp.einsum(
        "rglc,l->rgc",
        chosen.reshape(row_count, group_count, local_experts, CAP),
        mine_hot,
        precision=lax.Precision.HIGHEST,
    )
    combine_mine = jnp.einsum(
        "rgl,l->rg",
        combine.reshape(row_count, group_count, local_experts),
        mine_hot,
        precision=lax.Precision.HIGHEST,
    )
    placing = chosen_mine.reshape(row_count, group_count * CAP)
    outgoing = jnp.dot(
        placing.T.astype(jnp.bfloat16), tokens, preferred_element_type=jnp.float32
    ).astype(jnp.bfloat16)
    outgoing = outgoing.reshape(group_count, CAP, model_width)
    produced = expert_slice(
        lax.all_to_all(outgoing, "req", split_axis=0, concat_axis=0, tiled=True),
        expert_gate_up,
        expert_down,
    )
    returned = lax.all_to_all(produced, "req", split_axis=0, concat_axis=0, tiled=True)
    weighting = (chosen_mine * combine_mine[:, :, None]).reshape(row_count, group_count * CAP)
    routed = jnp.dot(
        weighting,
        returned.reshape(group_count * CAP, model_width),
        precision=lax.Precision.HIGHEST,
        preferred_element_type=jnp.float32,
    )
    routed = routed + lax.all_to_all(shared_out, "req", split_axis=0, concat_axis=1, tiled=True)
    final = lax.psum_scatter(routed, "head", scatter_dimension=1, tiled=True)
    slice_width = final.shape[1]
    own_resid = lax.dynamic_slice_in_dim(
        resid, lax.axis_index("head") * slice_width, slice_width, 1
    )
    return ((own_resid + final).astype(jnp.bfloat16), new_kv)


def solution(mesh):
    return jax.shard_map(
        local,
        mesh=mesh,
        in_specs=(
            P("req", None),
            P(),
            P(None, None, "head"),
            P(None, "head"),
            P("head", None),
            P("req", None, None, "head"),
            P("req", None, None, "head"),
            P("req"),
            P("req", None),
            P("req", None),
            P(),
            P(None, ("req", "head"), None),
            P(("req", "head"), None),
            P(None, "req", "head"),
            P("head", "req"),
            P(),
        ),
        out_specs=(P("req", "head"), P("req", None, "head")),
        check_vma=False,
    )
```

profile of v0, /device:TPU:0, one launch (start us, length us, event | category | flops | bytes accessed | tf_op | source)
XLA Modules:
  0.0 306.4 jit_solution(18246826656507924227)
XLA Ops:
  7.3 0.8 and_select_fusion
  8.1 8.8 %copy.43 = bf16[2048,3,512]{0,2,1:T(8,128)(2,1)} copy(bf16[2048,3,512]{2,0,1:T(8,128)(2,1)} %param.18) | data formatting | bytes 12582912 | tf_op args[2]
  17.1 4.5 %convolution_add_fusion = f32[8,1536]{1,0:T(8,128)S(1)} fusion(bf16[2048,1536]{0,1:T(8,128)(2,1)} %bitcast.145, bf16[8,2048]{1,0:T(8,128)(2,1)S(1)} %copy-done.4, f32[2048]{0:T(1024)S(1)} %copy-done.7, f32[8]{0:T(128)S(1)} %add_rsqrt_fusion.1, f32[1536]{0:T(1024)S(1)} %add.96), kind=kOutput, calls=%fused_computation.14 | convolution fusion | flops 50409472 | bytes 6387744 | tf_op jit(solution)/shard_map/dot_general | solution.py:106
  21.6 0.6 copy-done.5
  22.5 22.5 %fusion.80 = (bf16[8,1,2048,512]{3,2,1,0:T(8,128)(2,1)}, bf16[8,1,2048,512]{3,2,1,0:T(8,128)(2,1)}) fusion(bf16[8,2,2048,512]{3,2,1,0:T(8,128)(2,1)} %param.21), kind=kLoop, calls=%fused_computation.124 | loop fusion | bytes 67108864 | tf_op jit(solution)/shard_map/slice | solution.py:55
  45.0 21.6 %copy.77 = bf16[8,1,2048,512]{2,3,0,1:T(8,128)(2,1)} copy(bf16[8,1,2048,512]{3,2,1,0:T(8,128)(2,1)} %get-tuple-element.17) | data formatting | bytes 33554432 | tf_op jit(solution)/shard_map/reshape;squeeze | solution.py:41
  66.7 8.0 %fusion.58 = f32[8,4,1,2048]{3,2,1,0:T(1,128)S(1)} fusion(bf16[8,2048,4,128]{1,3,2,0:T(8,128)(2,1)} %bitcast.144, bf16[8,4,128,1]{2,0,1,3:T(8,128)(2,1)S(1)} %fusion.72), kind=kOutput, calls=%fused_computation.87 | convolution fusion | flops 16777216 | bytes 17047552 | tf_op jit(solution)/shard_map/rhd,rshd->rhs/dot_general | solution.py:42
  75.0 0.7 fusion.56
  76.1 0.3 fusion.29
  76.5 0.3 select_reduce_fusion
  76.8 0.7 select_bitcast_fusion
  77.5 23.7 %reshape_squeeze.14 = bf16[8,2048,4,128]{3,2,1,0:T(4,128)(2,1)} reshape(bf16[8,1,2048,512]{3,2,1,0:T(8,128)(2,1)} %get-tuple-element.16) | data formatting | bytes 33554432 | tf_op jit(solution)/shard_map/reshape;squeeze | solution.py:55
  101.4 8.3 %fusion = f32[8,4,1,128]{3,2,1,0:T(1,128)S(1)} fusion(bf16[8,2048,4,128]{3,2,1,0:T(4,128)(2,1)} %reshape_squeeze.14, bf16[8,4,2048,1]{2,0,1,3:T(8,128)(2,1)} %select_bitcast_fusion), kind=kOutput, calls=%fused_computation | convolution fusion | flops 16777216 | bytes 16924672 | tf_op jit(solution)/shard_map/rhs,rshd->rhd/dot_general | solution.py:63
  109.8 1.8 fusion.61
  111.6 0.5 iota_convert_fusion
  112.1 0.7 select_reduce_fusion.1
  112.8 0.8 copy.44
  113.5 0.7 copy.46
  114.3 3.2 %reduce_window_sum.14 = f32[8,8,4]{0,2,1:T(4,128)} reduce-window(f32[8,8,4]{0,2,1:T(4,128)S(1)} %bitcast.147, f32[]{:T(128)} %constant.67.clone.1), window={size=8x1x1 pad=7_0x0_0x0_0}, to_apply=%region_8.9 | reduce-window | flops 1792 | bytes 2052 | tf_op jit(solution)/shard_map/jit(cumsum)/reduce_window_sum | solution.py:170
  117.4 1.3 sub.46
  118.8 1.4 copy.45
  120.2 1.6 multiply_reduce_fusion
  121.8 1.5 copy.74
  123.3 0.7 copy.47
  124.2 0.8 broadcast_multiply_fusion
  124.9 20.5 %all-reduce.3.cloned.1.call-done = f32[8,2048]{1,0:T(8,128)} async-done(((f32[8,2048]{1,0:T(8,128)}), f32[8,2048]{1,0:T(8,128)}) %all-reduce.3.cloned.1.call-update) | async-done | bytes 65552 | tf_op jit(solution)/shard_map/psum | solution.py:144
  145.5 1.0 multiply_reduce_fusion.1
  146.4 0.6 copy-done.3
  147.0 0.8 multiply_convert_fusion
  147.8 32.8 %all_gather.3 = bf16[64,2048]{1,0:T(8,128)(2,1)} all-gather(bf16[8,2048]{1,0:T(8,128)(2,1)S(1)} %multiply_convert_fusion), channel_id=1, replica_groups=mesh['req'=8,'head'=4] {'req'}, dimensions={0}, use_global_device_ids=true | all-gather | bytes 294912 | tf_op jit(solution)/shard_map/all_gather | solution.py:146
  180.6 0.8 convolution_convert_fusion
  181.4 1.5 reshape.198
  182.9 5.4 %all-to-all-start = ((bf16[8,2,2048]{2,1,0:T(2,128)(2,1)}), bf16[8,2,2048]{2,1,0:T(2,128)(2,1)}, u32[]{:S(2)}, u32[]{:S(2)}) async-start(bf16[8,2,2048]{2,1,0:T(2,128)(2,1)} %reshape.198), calls=%async_computation | async-start | bytes 131072 | tf_op jit(solution)/shard_map/all_to_all | solution.py:193
  188.6 2.0 convolution_bitcast_fusion
  190.6 4.7 %all-to-all-done = bf16[8,2,2048]{2,1,0:T(2,128)(2,1)} async-done(((bf16[8,2,2048]{2,1,0:T(2,128)(2,1)}), bf16[8,2,2048]{2,1,0:T(2,128)(2,1)}, u32[]{:S(2)}, u32[]{:S(2)}) %all-to-all-start) | async-done | bytes 65568 | tf_op jit(solution)/shard_map/all_to_all | solution.py:193
  195.3 4.3 %fusion.6 = f32[8,2,1408]{2,0,1:T(8,128)S(1)} fusion(bf16[2,1408,2048]{2,1,0:T(8,128)(2,1)} %param.27, bf16[8,2,2048]{2,1,0:T(2,128)(2,1)} %all-to-all-done), kind=kOutput, calls=%fused_computation.6 | convolution fusion | flops 92274688 | bytes 5922816 | tf_op jit(solution)/shard_map/nkd,fd->nkf/dot_general | solution.py:72
  199.6 7.1 %fusion.2 = f32[8,2,2048]{2,0,1:T(8,128)S(1)} fusion(bf16[1408,2048]{1,0:T(8,128)(2,1)} %param.28, bf16[2,1408,2048]{2,1,0:T(8,128)(2,1)} %param.27, f32[8,2,1408]{2,0,1:T(8,128)S(1)} %fusion.6, bf16[8,2,2048]{2,1,0:T(2,128)(2,1)} %all-to-all-done), kind=kOutput, calls=%fused_computation.2 | convolution fusion | flops 184684544 | bytes 11821056 | tf_op jit(solution)/shard_map/nkf,fd->nkd/dot_general | solution.py:79
  206.6 0.8 copy.50
  207.4 3.4 %all-to-all-start.1 = ((f32[8,2,2048]{2,1,0:T(2,128)}), f32[8,2,2048]{2,1,0:T(2,128)S(1)}, u32[]{:S(2)}, u32[]{:S(2)}) async-start(f32[8,2,2048]{2,1,0:T(2,128)} %copy.50), calls=%async_computation.1 | async-start | bytes 262144 | tf_op jit(solution)/shard_map/all_to_all | solution.py:197
  210.9 0.3 fusion.21
  211.2 57.6 %all-reduce.5.cloned.1.call-done = f32[2,64,1408]{2,1,0:T(8,128)} async-done(((f32[2,64,1408]{2,1,0:T(8,128)}), f32[2,64,1408]{2,1,0:T(8,128)}) %all-reduce.5.cloned.1.call-update) | async-done | bytes 720912 | tf_op jit(solution)/shard_map/psum | solution.py:154
  268.7 1.4 fusion.17
  270.1 10.4 %all_to_all.29 = f32[8,8,256]{2,1,0:T(8,128)S(1)} all-to-all(f32[8,8,256]{2,1,0:T(8,128)S(1)} %fusion.17), channel_id=1, replica_groups=mesh['req'=8,'head'=4] {'req'}, dimensions={0} | all-to-all | bytes 131072 | tf_op jit(solution)/shard_map/all_to_all | solution.py:205
  280.5 0.9 fusion.16
  281.4 0.7 fusion.69
  282.2 0.6 copy.53
  282.8 15.7 %reduce-scatter.2.cloned.1.call-done = f32[8,512]{1,0:T(8,128)} async-done(((f32[8,2048]{1,0:T(8,128)}), f32[8,512]{1,0:T(8,128)}) %reduce-scatter.2.cloned.1.call-update) | async-done | bytes 16400 | tf_op jit(solution)/shard_map/reduce_scatter | solution.py:206
  298.5 1.3 add_convert_fusion
  (58 shorter events, 2.0 us)
Async XLA Ops:
  7.2 102.6 %copy-start = (bf16[512,2048]{1,0:T(8,128)(2,1)S(1)}, bf16[512,2048]{1,0:T(8,128)(2,1)}, u32[]{:S(2)}) copy-start(bf16[512,2048]{1,0:T(8,128)(2,1)} %param.20) | copy-start | bytes 6291460
  7.2 9.7 %copy-start.8 = (f32[3,512]{1,0:T(4,128)S(1)}, f32[3,512]{1,0:T(4,128)}, u32[]{:S(2)}) copy-start(f32[3,512]{1,0:T(4,128)} %param.19) | copy-start | bytes 18436
  7.2 9.7 %copy-start.4 = (bf16[8,2048]{1,0:T(8,128)(2,1)S(1)}, bf16[8,2048]{1,0:T(8,128)(2,1)}, u32[]{:S(2)}) copy-start(bf16[8,2048]{1,0:T(8,128)(2,1)} %param.16) | copy-start | bytes 98308
  7.2 9.9 %copy-start.7 = (f32[2048]{0:T(1024)S(1)}, f32[2048]{0:T(1024)}, u32[]{:S(2)}) copy-start(f32[2048]{0:T(1024)} %param.17) | copy-start | bytes 24580
  7.2 138.2 %all-reduce.3.cloned.1.call-start = ((), (), s32[]{:S(2)}) async-start(), calls=%async_computation.4 | async-start | bytes 131072 | tf_op jit(solution)/shard_map/psum | solution.py:144
  21.6 0.6 copy-start.5
  66.6 8.1 %copy-start.12 = (bf16[8,2,4,512]{3,2,1,0:T(4,128)(2,1)S(1)}, bf16[8,2,4,512]{3,2,1,0:T(4,128)(2,1)}, u32[]{:S(2)}) copy-start(bf16[8,2,4,512]{3,2,1,0:T(4,128)(2,1)} %param.22) | copy-start | bytes 196612
  101.4 10.7 %copy-start.9 = (f32[8,4]{0,1:T(4,128)S(1)}, f32[8,4]{0,1:T(4,128)}, u32[]{:S(2)}) copy-start(f32[8,4]{0,1:T(4,128)} %param.25) | copy-start | bytes 388
  101.4 10.7 %copy-start.10 = (s32[8,4]{0,1:T(4,128)S(1)}, s32[8,4]{0,1:T(4,128)}, u32[]{:S(2)}) copy-start(s32[8,4]{0,1:T(4,128)} %param.24) | copy-start | bytes 388
  101.4 87.1 %copy-start.1 = (bf16[2,256,1408]{2,1,0:T(8,128)(2,1)S(1)}, bf16[2,256,1408]{2,1,0:T(8,128)(2,1)}, u32[]{:S(2)}) copy-start(bf16[2,256,1408]{2,1,0:T(8,128)(2,1)} %param.29) | copy-start | bytes 4325380
  146.4 0.6 copy-start.3
  182.9 12.4 %all-to-all-start = ((bf16[8,2,2048]{2,1,0:T(2,128)(2,1)}), bf16[8,2,2048]{2,1,0:T(2,128)(2,1)}, u32[]{:S(2)}, u32[]{:S(2)}) async-start(bf16[8,2,2048]{2,1,0:T(2,128)(2,1)} %reshape.198), calls=%async_computation | async-start | bytes 131072 | tf_op jit(solution)/shard_map/all_to_all | solution.py:193
  188.3 80.4 %all-reduce.5.cloned.1.call-start = ((), (), s32[]{:S(2)}) async-start(), calls=%async_computation.5 | async-start | bytes 1441792 | tf_op jit(solution)/shard_map/psum | solution.py:154
  190.6 20.3 %copy-start.2 = (bf16[64,2048]{1,0:T(8,128)(2,1)S(1)}, bf16[64,2048]{1,0:T(8,128)(2,1)}, u32[]{:S(2)}) copy-start(bf16[64,2048]{1,0:T(8,128)(2,1)} %all_gather.3) | copy-start | bytes 786436
  190.6 20.3 %copy-start.13 = (f32[2048]{0:T(1024)S(1)}, f32[2048]{0:T(1024)}, u32[]{:S(2)}) copy-start(f32[2048]{0:T(1024)} %param.31) | copy-start | bytes 24580
  190.6 78.1 %copy-start.11 = (bf16[1408,256]{1,0:T(8,128)(2,1)S(1)}, bf16[1408,256]{1,0:T(8,128)(2,1)}, u32[]{:S(2)}) copy-start(bf16[1408,256]{1,0:T(8,128)(2,1)} %param.30) | copy-start | bytes 2162692
  190.6 91.5 %copy-start.6 = (bf16[8,4,128]{2,0,1:T(8,128)(2,1)S(1)}, bf16[8,4,128]{2,0,1:T(8,128)(2,1)}, u32[]{:S(2)}) copy-start(bf16[8,4,128]{2,0,1:T(8,128)(2,1)} %get-tuple-element.15) | copy-start | bytes 24580
  207.4 62.7 %all-to-all-start.1 = ((f32[8,2,2048]{2,1,0:T(2,128)}), f32[8,2,2048]{2,1,0:T(2,128)S(1)}, u32[]{:S(2)}, u32[]{:S(2)}) async-start(f32[8,2,2048]{2,1,0:T(2,128)} %copy.50), calls=%async_computation.1 | async-start | bytes 262144 | tf_op jit(solution)/shard_map/all_to_all | solution.py:197
  210.8 87.7 %reduce-scatter.2.cloned.1.call-start = ((), (), s32[]{:S(2)}) async-start(), calls=%async_computation.6 | async-start | bytes 81920 | tf_op jit(solution)/shard_map/reduce_scatter | solution.py:206
Sparse Core Ops, SparseCore 0:
  111.7 33.7 all-reduce.2
  193.1 75.6 all-reduce.4
  281.6 16.9 reduce-scatter.1
where the time goes:
time: 309 us; the launch traced here: 306 us
  waiting for transfers between devices  98.6 us (32%)
  local copies, waits for them, and re-layouts  86.9 us (28%)
  blocking collectives  43.2 us (14%)
  matrix products  39.7 us (13%)
  other arithmetic  14.9 us (5%)
  between operations  14 us (5%)
  starting transfers between devices  9.11 us (3%)
    psum x1, waiting for transfers between devices, local(): shared_terms = lax.psum(shared_terms, 'req')  57.6 us
    all_gather x1, blocking collectives, local(): all_tokens = lax.all_gather(tokens, 'req', axis=0, tiled=True)  32.8 us
    another operation x1, local copies, waits for them, and re-layouts, block_values(): window_cache[:, 1].reshape(row_count, block_size, head_count, head_depth)  23.7 us
    slice x1, local copies, waits for them, and re-layouts, block_values(): window_cache[:, 1].reshape(row_count, block_size, head_count, head_depth)  22.5 us
    another operation x1, local copies, waits for them, and re-layouts, block_scores(): window_cache[:, 0].reshape(row_count, block_size, head_count, head_depth)  21.6 us
    psum x1, waiting for transfers between devices, local(): resid = hidden_state.astype(jnp.float32) + lax.psum(attend_part, 'head')  20.5 us
    reduce_scatter x1, waiting for transfers between devices, local(): final = lax.psum_scatter(routed, 'head', scatter_dimension=1, tiled=True)  15.7 us
    unnamed x30, local copies, waits for them, and re-layouts  10.8 us
  transfers between devices with their start and end apart: 5, of which 4 were waited for; matrix products, arithmetic and copies ran while one was open for 10% of the time, Pallas kernels for 0%

commit v1 on v0

--- a/solution.py
+++ b/solution.py
@@ -143,7 +143,14 @@
     attend_part = jnp.dot(attended, output_weight, preferred_element_type=jnp.float32)
     resid = hidden_state.astype(jnp.float32) + lax.psum(attend_part, "head")
     tokens = rms_scale(resid, mixture_gain).astype(jnp.bfloat16)
-    all_tokens = lax.all_gather(tokens, "req", axis=0, tiled=True)
+    ways, here = (lax.axis_size("req"), lax.axis_index("req"))
+    all_tokens, reach = (tokens, 1)
+    while reach < ways:
+        theirs = lax.ppermute(all_tokens, "req", [(d, d ^ reach) for d in range(ways)])
+        mine_first = jnp.concatenate([all_tokens, theirs], axis=0)
+        theirs_first = jnp.concatenate([theirs, all_tokens], axis=0)
+        all_tokens = jnp.where(here & reach == 0, mine_first, theirs_first)
+        reach = 2 * reach
     group_index = lax.axis_index("req")
     group_count = lax.axis_size("req")
     row_width = shared_gate_up.shape[1]

time: 309 us -> 293 us (0.948)
  blocking collectives: 43.2 us -> 10.4 us
  other arithmetic: 14.9 us -> 20.1 us
  starting transfers between devices: 9.11 us -> 14.1 us
  waiting for transfers between devices: 98.6 us -> 102 us
  matrix products: 39.7 us -> 42.9 us
    all_gather x1 -> x0, blocking collectives: 32.8 us -> none  [local(): all_tokens = lax.all_gather(tokens, 'req', axis=0, tiled=True)]
    ppermute x0 -> x3, starting transfers between devices: none -> 5.65 us  [local(): lax.ppermute(all_tokens, 'req', [(d, d ^ reach) for d in range(ways)])]
    select_n x0 -> x3, other arithmetic: none -> 4.25 us  [local(): all_tokens = jnp.where(here & reach == 0, mine_first, theirs_first)]
    psum x1, waiting for transfers between devices: 57.6 us -> 61.2 us  [local(): shared_terms = lax.psum(shared_terms, 'req')]
  transfers between devices with their start and end apart: 5 -> 8, of which waited for: 4 -> 5; matrix products, arithmetic and copies ran while one was open for 10% -> 12% of each run, Pallas kernels for 0% -> 0%
where the time goes in v1:
time: 293 us; the launch traced here: 290 us
  waiting for transfers between devices  102 us (35%)
  local copies, waits for them, and re-layouts  87 us (30%)
  matrix products  42.9 us (15%)
  other arithmetic  20.1 us (7%)
  starting transfers between devices  14.1 us (5%)
  between operations  14 us (5%)
  blocking collectives  10.4 us (4%)
    psum x1, waiting for transfers between devices, local(): shared_terms = lax.psum(shared_terms, 'req')  61.2 us
    another operation x1, local copies, waits for them, and re-layouts, block_values(): window_cache[:, 1].reshape(row_count, block_size, head_count, head_depth)  23.7 us
    slice x1, local copies, waits for them, and re-layouts, block_values(): window_cache[:, 1].reshape(row_count, block_size, head_count, head_depth)  22.5 us
    another operation x1, local copies, waits for them, and re-layouts, block_scores(): window_cache[:, 0].reshape(row_count, block_size, head_count, head_depth)  21.6 us
    psum x1, waiting for transfers between devices, local(): resid = hidden_state.astype(jnp.float32) + lax.psum(attend_part, 'head')  20.8 us
    reduce_scatter x1, waiting for transfers between devices, local(): final = lax.psum_scatter(routed, 'head', scatter_dimension=1, tiled=True)  15.7 us
    unnamed x30, local copies, waits for them, and re-layouts  11.4 us
    all_to_all x1, blocking collectives, local(): lax.all_to_all(shared_out, 'req', split_axis=0, concat_axis=1, tiled=True)  10.4 us
  transfers between devices with their start and end apart: 8, of which 5 were waited for; matrix products, arithmetic and copies ran while one was open for 12% of the time, Pallas kernels for 0%

profile of v1, /device:TPU:0, one launch (start us, length us, event | category | flops | bytes accessed | tf_op | source)
XLA Modules:
  0.0 290.2 jit_solution(14965054002167410368)
XLA Ops:
  7.3 0.8 and_select_fusion
  8.1 8.8 %copy.43 = bf16[2048,3,512]{0,2,1:T(8,128)(2,1)} copy(bf16[2048,3,512]{2,0,1:T(8,128)(2,1)} %param.18) | data formatting | bytes 12582912 | tf_op args[2]
  17.1 4.5 %convolution_add_fusion = f32[8,1536]{1,0:T(8,128)S(1)} fusion(bf16[2048,1536]{0,1:T(8,128)(2,1)} %bitcast.145, bf16[8,2048]{1,0:T(8,128)(2,1)S(1)} %copy-done.5, f32[2048]{0:T(1024)S(1)} %copy-done.8, f32[8]{0:T(128)S(1)} %add_rsqrt_fusion.1, f32[1536]{0:T(1024)S(1)} %add.96), kind=kOutput, calls=%fused_computation.14 | convolution fusion | flops 50409472 | bytes 6387744 | tf_op jit(solution)/shard_map/dot_general | solution.py:106
  22.5 22.5 %fusion.80 = (bf16[8,1,2048,512]{3,2,1,0:T(8,128)(2,1)}, bf16[8,1,2048,512]{3,2,1,0:T(8,128)(2,1)}) fusion(bf16[8,2,2048,512]{3,2,1,0:T(8,128)(2,1)} %param.21), kind=kLoop, calls=%fused_computation.127 | loop fusion | bytes 67108864 | tf_op jit(solution)/shard_map/slice | solution.py:55
  45.0 21.6 %copy.77 = bf16[8,1,2048,512]{2,3,0,1:T(8,128)(2,1)} copy(bf16[8,1,2048,512]{3,2,1,0:T(8,128)(2,1)} %get-tuple-element.17) | data formatting | bytes 33554432 | tf_op jit(solution)/shard_map/reshape;squeeze | solution.py:41
  66.7 8.0 %fusion.58 = f32[8,4,1,2048]{3,2,1,0:T(1,128)S(1)} fusion(bf16[8,2048,4,128]{1,3,2,0:T(8,128)(2,1)} %bitcast.144, bf16[8,4,128,1]{2,0,1,3:T(8,128)(2,1)S(1)} %fusion.72), kind=kOutput, calls=%fused_computation.90 | convolution fusion | flops 16777216 | bytes 17047552 | tf_op jit(solution)/shard_map/rhd,rshd->rhs/dot_general | solution.py:42
  75.0 0.7 fusion.56
  76.8 23.7 %reshape_squeeze.14 = bf16[8,2048,4,128]{3,2,1,0:T(4,128)(2,1)} reshape(bf16[8,1,2048,512]{3,2,1,0:T(8,128)(2,1)} %get-tuple-element.16) | data formatting | bytes 33554432 | tf_op jit(solution)/shard_map/reshape;squeeze | solution.py:55
  100.8 9.2 %fusion = f32[8,4,1,128]{3,2,1,0:T(1,128)S(1)} fusion(bf16[8,2048,4,128]{3,2,1,0:T(4,128)(2,1)} %reshape_squeeze.14, bf16[8,4,2048,1]{2,0,1,3:T(8,128)(2,1)S(1)} %select_bitcast_fusion), kind=kOutput, calls=%fused_computation | convolution fusion | flops 16777216 | bytes 16924672 | tf_op jit(solution)/shard_map/rhs,rshd->rhd/dot_general | solution.py:63
  110.0 1.9 fusion.61
  113.1 0.8 copy.44
  113.9 0.7 copy.46
  114.6 3.2 %reduce_window_sum.14 = f32[8,8,4]{0,2,1:T(4,128)} reduce-window(f32[8,8,4]{0,2,1:T(4,128)S(1)} %bitcast.147, f32[]{:T(128)} %constant.69.clone.1), window={size=8x1x1 pad=7_0x0_0x0_0}, to_apply=%region_8.9 | reduce-window | flops 1792 | bytes 2052 | tf_op jit(solution)/shard_map/jit(cumsum)/reduce_window_sum | solution.py:177
  117.8 1.3 sub.46
  119.1 1.4 copy.45
  121.1 0.7 copy.47
  121.8 0.7 fusion.70
  122.6 1.6 multiply_reduce_fusion
  124.2 0.9 copy.74
  125.1 20.8 %all-reduce.3.cloned.1.call-done = f32[8,2048]{1,0:T(8,128)} async-done(((f32[8,2048]{1,0:T(8,128)}), f32[8,2048]{1,0:T(8,128)}) %all-reduce.3.cloned.1.call-update) | async-done | bytes 65552 | tf_op jit(solution)/shard_map/psum | solution.py:144
  145.8 1.0 multiply_reduce_fusion.1
  147.4 1.4 multiply_convert_fusion
  148.8 1.5 collective-permute-start
  150.3 1.3 broadcast_multiply_fusion
  151.6 1.5 collective-permute-done
  153.0 1.5 maximum_select_fusion.2
  154.5 1.5 collective-permute-start.1
  156.0 1.5 convolution_convert_fusion
  157.5 1.5 reshape.198
  159.0 4.6 %all-to-all-start = ((bf16[8,2,2048]{2,1,0:T(2,128)(2,1)}), bf16[8,2,2048]{2,1,0:T(2,128)(2,1)}, u32[]{:S(2)}, u32[]{:S(2)}) async-start(bf16[8,2,2048]{2,1,0:T(2,128)(2,1)} %reshape.198), calls=%async_computation | async-start | bytes 131072 | tf_op jit(solution)/shard_map/all_to_all | solution.py:200
  163.8 1.6 maximum_select_fusion.1
  165.5 2.7 collective-permute-start.2
  168.2 2.5 all-to-all-done
  170.6 4.9 %fusion.6 = f32[8,2,1408]{2,0,1:T(8,128)} fusion(bf16[2,1408,2048]{2,1,0:T(8,128)(2,1)} %param.27, bf16[8,2,2048]{2,1,0:T(2,128)(2,1)} %all-to-all-done), kind=kOutput, calls=%fused_computation.6 | convolution fusion | flops 92274688 | bytes 5922816 | tf_op jit(solution)/shard_map/nkd,fd->nkf/dot_general | solution.py:72
  175.5 1.2 maximum_select_fusion
  176.7 0.7 copy-done.2
  177.4 1.2 convolution_bitcast_fusion
  178.7 7.3 %fusion.2 = f32[8,2,2048]{2,0,1:T(8,128)S(1)} fusion(bf16[1408,2048]{1,0:T(8,128)(2,1)} %param.28, bf16[2,1408,2048]{2,1,0:T(8,128)(2,1)} %param.27, f32[8,2,1408]{2,0,1:T(8,128)} %fusion.6, bf16[8,2,2048]{2,1,0:T(2,128)(2,1)} %all-to-all-done), kind=kOutput, calls=%fused_computation.2 | convolution fusion | flops 184684544 | bytes 11821056 | tf_op jit(solution)/shard_map/nkf,fd->nkd/dot_general | solution.py:79
  186.0 0.8 copy.50
  186.7 3.5 %all-to-all-start.1 = ((f32[8,2,2048]{2,1,0:T(2,128)}), f32[8,2,2048]{2,1,0:T(2,128)S(1)}, u32[]{:S(2)}, u32[]{:S(2)}) async-start(f32[8,2,2048]{2,1,0:T(2,128)} %copy.50), calls=%async_computation.1 | async-start | bytes 262144 | tf_op jit(solution)/shard_map/all_to_all | solution.py:204
  190.3 1.0 fusion.21
  191.3 61.2 %all-reduce.5.cloned.1.call-done = f32[2,64,1408]{2,1,0:T(8,128)} async-done(((f32[2,64,1408]{2,1,0:T(8,128)}), f32[2,64,1408]{2,1,0:T(8,128)}) %all-reduce.5.cloned.1.call-update) | async-done | bytes 720912 | tf_op jit(solution)/shard_map/psum | solution.py:161
  252.5 1.4 fusion.17
  253.9 10.4 %all_to_all.29 = f32[8,8,256]{2,1,0:T(8,128)S(1)} all-to-all(f32[8,8,256]{2,1,0:T(8,128)S(1)} %fusion.17), channel_id=1, replica_groups=mesh['req'=8,'head'=4] {'req'}, dimensions={0} | all-to-all | bytes 131072 | tf_op jit(solution)/shard_map/all_to_all | solution.py:212
  264.3 0.9 fusion.16
  265.2 0.7 fusion.69
  266.6 15.7 %reduce-scatter.2.cloned.1.call-done = f32[8,512]{1,0:T(8,128)} async-done(((f32[8,2048]{1,0:T(8,128)}), f32[8,512]{1,0:T(8,128)}) %reduce-scatter.2.cloned.1.call-update) | async-done | bytes 16400 | tf_op jit(solution)/shard_map/reduce_scatter | solution.py:213
  282.3 1.3 add_convert_fusion
  (66 shorter events, 6.1 us)
Async XLA Ops:
  7.2 102.9 %copy-start = (bf16[512,2048]{1,0:T(8,128)(2,1)S(1)}, bf16[512,2048]{1,0:T(8,128)(2,1)}, u32[]{:S(2)}) copy-start(bf16[512,2048]{1,0:T(8,128)(2,1)} %param.20) | copy-start | bytes 6291460
  7.2 9.7 %copy-start.9 = (f32[3,512]{1,0:T(4,128)S(1)}, f32[3,512]{1,0:T(4,128)}, u32[]{:S(2)}) copy-start(f32[3,512]{1,0:T(4,128)} %param.19) | copy-start | bytes 18436
  7.2 9.7 %copy-start.5 = (bf16[8,2048]{1,0:T(8,128)(2,1)S(1)}, bf16[8,2048]{1,0:T(8,128)(2,1)}, u32[]{:S(2)}) copy-start(bf16[8,2048]{1,0:T(8,128)(2,1)} %param.16) | copy-start | bytes 98308
  7.2 9.9 %copy-start.8 = (f32[2048]{0:T(1024)S(1)}, f32[2048]{0:T(1024)}, u32[]{:S(2)}) copy-start(f32[2048]{0:T(1024)} %param.17) | copy-start | bytes 24580
  7.2 138.6 %all-reduce.3.cloned.1.call-start = ((), (), s32[]{:S(2)}) async-start(), calls=%async_computation.4 | async-start | bytes 131072 | tf_op jit(solution)/shard_map/psum | solution.py:144
  21.6 0.6 copy-start.6
  66.6 8.1 %copy-start.13 = (bf16[8,2,4,512]{3,2,1,0:T(4,128)(2,1)S(1)}, bf16[8,2,4,512]{3,2,1,0:T(4,128)(2,1)}, u32[]{:S(2)}) copy-start(bf16[8,2,4,512]{3,2,1,0:T(4,128)(2,1)} %param.22) | copy-start | bytes 196612
  100.8 11.7 %copy-start.10 = (f32[8,4]{0,1:T(4,128)S(1)}, f32[8,4]{0,1:T(4,128)}, u32[]{:S(2)}) copy-start(f32[8,4]{0,1:T(4,128)} %param.25) | copy-start | bytes 388
  100.8 11.7 %copy-start.11 = (s32[8,4]{0,1:T(4,128)S(1)}, s32[8,4]{0,1:T(4,128)}, u32[]{:S(2)}) copy-start(s32[8,4]{0,1:T(4,128)} %param.24) | copy-start | bytes 388
  110.0 67.4 %copy-start.1 = (bf16[2,256,1408]{2,1,0:T(8,128)(2,1)S(1)}, bf16[2,256,1408]{2,1,0:T(8,128)(2,1)}, u32[]{:S(2)}) copy-start(bf16[2,256,1408]{2,1,0:T(8,128)(2,1)} %param.29) | copy-start | bytes 4325380
  146.8 0.6 copy-start.4
  148.8 4.2 %collective-permute-start = (bf16[8,2048]{1,0:T(8,128)(2,1)}, bf16[8,2048]{1,0:T(8,128)(2,1)}, u32[]{:S(2)}, u32[]{:S(2)}) collective-permute-start(bf16[8,2048]{1,0:T(8,128)(2,1)} %multiply_convert_fusion), channel_id=1, source_target_pairs={{0,4},{4,0},{8,12},{12,8},{16,20},{20,16},{24,28},{28,24},{1,5},{5... | collective-permute-start | bytes 98312 | tf_op jit(solution)/shard_map/ppermute | solution.py:149
  154.5 9.3 %collective-permute-start.1 = (bf16[16,2048]{1,0:T(8,128)(2,1)}, bf16[16,2048]{1,0:T(8,128)(2,1)}, u32[]{:S(2)}, u32[]{:S(2)}) collective-permute-start(bf16[16,2048]{1,0:T(8,128)(2,1)} %maximum_select_fusion.2), channel_id=1, source_target_pairs={{0,8},{4,12},{8,0},{12,4},{16,24},{20,28},{24,16},{28,20},{1,9},{5... | collective-permute-start | bytes 196616 | tf_op jit(solution)/shard_map/ppermute | solution.py:149
  159.0 11.6 %all-to-all-start = ((bf16[8,2,2048]{2,1,0:T(2,128)(2,1)}), bf16[8,2,2048]{2,1,0:T(2,128)(2,1)}, u32[]{:S(2)}, u32[]{:S(2)}) async-start(bf16[8,2,2048]{2,1,0:T(2,128)(2,1)} %reshape.198), calls=%async_computation | async-start | bytes 131072 | tf_op jit(solution)/shard_map/all_to_all | solution.py:200
  163.6 88.9 %all-reduce.5.cloned.1.call-start = ((), (), s32[]{:S(2)}) async-start(), calls=%async_computation.5 | async-start | bytes 1441792 | tf_op jit(solution)/shard_map/psum | solution.py:161
  165.5 10.1 %collective-permute-start.2 = (bf16[32,2048]{1,0:T(8,128)(2,1)}, bf16[32,2048]{1,0:T(8,128)(2,1)}, u32[]{:S(2)}, u32[]{:S(2)}) collective-permute-start(bf16[32,2048]{1,0:T(8,128)(2,1)} %maximum_select_fusion.1), channel_id=1, source_target_pairs={{0,16},{4,20},{8,24},{12,28},{16,0},{20,4},{24,8},{28,12},{1,17},{... | collective-permute-start | bytes 393224 | tf_op jit(solution)/shard_map/ppermute | solution.py:149
  175.5 90.4 %copy-start.7 = (bf16[8,4,128]{2,0,1:T(8,128)(2,1)S(1)}, bf16[8,4,128]{2,0,1:T(8,128)(2,1)}, u32[]{:S(2)}) copy-start(bf16[8,4,128]{2,0,1:T(8,128)(2,1)} %get-tuple-element.15) | copy-start | bytes 24580
  176.7 0.7 copy-start.2
  178.6 11.7 %copy-start.3 = (bf16[64,2048]{1,0:T(8,128)(2,1)S(1)}, bf16[64,2048]{1,0:T(8,128)(2,1)}, u32[]{:S(2)}) copy-start(bf16[64,2048]{1,0:T(8,128)(2,1)} %copy-done.2) | copy-start | bytes 786436
  178.6 73.9 %copy-start.12 = (bf16[1408,256]{1,0:T(8,128)(2,1)S(1)}, bf16[1408,256]{1,0:T(8,128)(2,1)}, u32[]{:S(2)}) copy-start(bf16[1408,256]{1,0:T(8,128)(2,1)} %param.30) | copy-start | bytes 2162692
  186.7 67.2 %all-to-all-start.1 = ((f32[8,2,2048]{2,1,0:T(2,128)}), f32[8,2,2048]{2,1,0:T(2,128)S(1)}, u32[]{:S(2)}, u32[]{:S(2)}) async-start(f32[8,2,2048]{2,1,0:T(2,128)} %copy.50), calls=%async_computation.1 | async-start | bytes 262144 | tf_op jit(solution)/shard_map/all_to_all | solution.py:204
  190.3 92.1 %reduce-scatter.2.cloned.1.call-start = ((), (), s32[]{:S(2)}) async-start(), calls=%async_computation.6 | async-start | bytes 81920 | tf_op jit(solution)/shard_map/reduce_scatter | solution.py:213
Sparse Core Ops, SparseCore 0:
  112.1 33.7 all-reduce.2
  178.8 73.6 all-reduce.4
  265.4 16.9 reduce-scatter.1
